TPU v7x, 32 devices: a whole 2x2x4 slice. The times are simulated.
32 devices in a mesh: dp: 16 (over z, y, x), grp: 2 (over core).
Axes of the slice: x: 2, y: 2, z: 4, core: 2. Of those that a mesh axis runs over, the one named last changes fastest.
Arguments:
- query_features: bfloat16 [32768, 512], P(('dp', 'grp')), may hold values from -256 to 256
- query_weights: bfloat16 [32768], P(('dp', 'grp')), may hold values from 0.5 to 13.5, as said below
- positive_index: int32 [32768], P(('dp', 'grp')), may hold values from 0 to 511
- item_features: bfloat16 [512, 512], P(('dp', 'grp')), may hold values from -6 to 6
- item_ids: int32 [512], P(('dp', 'grp')), may hold values from 0 to 255
- item_logq: bfloat16 [512], P(('dp', 'grp')), may hold values from -14 to -11
- query_w_in: bfloat16 [512, 1024], replicated, may hold values from -0.25 to 0.25
- query_w_out: bfloat16 [1024, 256], replicated, may hold values from -0.1875 to 0.1875
- item_w_in: bfloat16 [512, 1024], replicated, may hold values from -0.25 to 0.25
- item_w_out: bfloat16 [1024, 256], replicated, may hold values from -0.1875 to 0.1875
Outputs:
- grad_query_w_in: float32 [512, 1024], replicated
- grad_query_w_out: float32 [1024, 256], replicated
- grad_item_w_in: float32 [512, 1024], replicated
- grad_item_w_out: float32 [1024, 256], replicated
Inputs may be any that keep to these rules, and one draw needn't show every extreme that they name: `query_weights`: positive weights. `item_ids`: an id may occur several times in the sample set.
All inputs are finite; a program needn't handle non-finite values.
Results may differ from a plain program's by a relative error of at most 0.013.
Values may be sent and summed in bfloat16 or wider, within the bound.
A program may use at most 128 MiB of HBM per device.

v0:
```python
import jax
import jax.numpy as jnp
from jax import lax
from jax.sharding import PartitionSpec as P

score_scale = 0.25
loss_scale = 1024.0


def silu_slope(values):
    gate = jax.nn.sigmoid(values)
    return gate * (1.0 + values * (1.0 - gate))


def tower(features, weight_in, weight_out):
    pre_act = jnp.dot(features, weight_in, preferred_element_type=jnp.float32)
    hidden = jax.nn.silu(pre_act).astype(jnp.bfloat16)
    embedding = jnp.dot(hidden, weight_out, preferred_element_type=jnp.float32).astype(jnp.bfloat16)
    return (pre_act, hidden, embedding)


def tower_back(features, pre_act, hidden, weight_out, embed_grad):
    grad_out = jnp.dot(hidden.T, embed_grad, preferred_element_type=jnp.float32)
    hidden_grad = jnp.dot(embed_grad, weight_out.T, preferred_element_type=jnp.float32)
    pre_grad = (hidden_grad * silu_slope(pre_act)).astype(jnp.bfloat16)
    grad_in = jnp.dot(features.T, pre_grad, preferred_element_type=jnp.float32)
    return (grad_in, grad_out)


def item_scores(query_rows, items, item_bias, item_codes, columns, positives, pos_codes):
    raw_scores = lax.dot_general(
        query_rows, items, (((1,), (1,)), ((), ())), preferred_element_type=jnp.float32
    )
    scores = score_scale * raw_scores - item_bias.astype(jnp.float32)[None, :]
    masked_hits = (item_codes[None, :] == pos_codes[:, None]) & (
        columns[None, :] != positives[:, None]
    )
    return jnp.where(masked_hits, -jnp.inf, scores)


def partial_stats(scores):
    row_max = jnp.maximum(jnp.max(scores, axis=1), -1e30)
    row_sum = jnp.sum(jnp.exp(scores - row_max[:, None]), axis=1)
    return (row_max, row_sum)


def finish(scores, row_max, row_sum, columns, positives, weights):
    probability = jnp.exp(scores - row_max[:, None]) / row_sum[:, None]
    target = (columns[None, :] == positives[:, None]).astype(jnp.float32)
    return (weights.astype(jnp.float32)[:, None] * (probability - target)).astype(jnp.bfloat16)


def positive_codes(every_code, positives):
    slots = jnp.arange(every_code.shape[0], dtype=jnp.int32)
    return jnp.sum(jnp.where(positives[:, None] == slots[None, :], every_code[None, :], 0), axis=1)


def on_device(
    query_features,
    query_weights,
    positive_index,
    item_features,
    item_ids,
    item_logq,
    query_w_in,
    query_w_out,
    item_w_in,
    item_w_out,
):
    weight_part = jnp.sum(query_weights.astype(jnp.float32))
    weight_total = lax.psum(weight_part, ("dp", "grp"))
    query_pre, query_hidden, query_embed = tower(query_features, query_w_in, query_w_out)
    item_pre, item_hidden, item_embed = tower(item_features, item_w_in, item_w_out)
    items_all, bias_all, codes_all = (
        lax.all_gather(item_embed, ("dp", "grp"), axis=0, tiled=True),
        lax.all_gather(item_logq, ("dp", "grp"), axis=0, tiled=True),
        lax.all_gather(item_ids, ("dp", "grp"), axis=0, tiled=True),
    )
    columns = jnp.arange(items_all.shape[0], dtype=jnp.int32)
    pos_codes = positive_codes(codes_all, positive_index)
    scores = item_scores(
        query_embed, items_all, bias_all, codes_all, columns, positive_index, pos_codes
    )
    row_max, row_sum = partial_stats(scores)
    dlogit = finish(scores, row_max, row_sum, columns, positive_index, query_weights)
    query_grad = (
        score_scale * jnp.dot(dlogit, items_all, preferred_element_type=jnp.float32)
    ).astype(jnp.bfloat16)
    item_grad = lax.psum_scatter(
        score_scale
        * lax.dot_general(
            dlogit, query_embed, (((0,), (0,)), ((), ())), preferred_element_type=jnp.float32
        ),
        ("dp", "grp"),
        scatter_dimension=0,
        tiled=True,
    ).astype(jnp.bfloat16)
    query_in_part, query_out_part = tower_back(
        query_features, query_pre, query_hidden, query_w_out, query_grad
    )
    item_in_part, item_out_part = tower_back(
        item_features, item_pre, item_hidden, item_w_out, item_grad
    )
    query_in_sum, query_out_sum, item_in_sum, item_out_sum = lax.psum(
        (query_in_part, query_out_part, item_in_part, item_out_part), ("dp", "grp")
    )
    factor = loss_scale / weight_total
    return (
        query_in_sum * factor,
        query_out_sum * factor,
        item_in_sum * factor,
        item_out_sum * factor,
    )


def solution(mesh):
    in_specs = (
        P(("dp", "grp"), None),
        P(("dp", "grp")),
        P(("dp", "grp")),
        P(("dp", "grp"), None),
        P(("dp", "grp")),
        P(("dp", "grp")),
        P(),
        P(),
        P(),
        P(),
    )
    out_specs = (P(), P(), P(), P())
    return jax.shard_map(
        on_device, mesh=mesh, in_specs=in_specs, out_specs=out_specs, check_vma=False
    )
```

profile of v0, /device:TPU:0, one launch (start us, length us, event | category | flops | bytes accessed | tf_op | source)
XLA Modules:
  0.0 457.4 jit_solution(10545431475410207212)
XLA Ops:
  7.2 0.0 reduce-scatter.2.cloned.1.call-start
  7.2 1.6 fusion.16
  8.8 1.2 convolution_convert_fusion.1
  10.0 43.9 %all_gather.10 = bf16[512,256]{1,0:T(8,128)(2,1)S(1)} all-gather(bf16[16,256]{1,0:T(8,128)(2,1)S(1)} %convolution_convert_fusion.1), channel_id=1, replica_groups=mesh['dp'=16,'grp'=2] {'dp','grp'}, dimensions={0}, use_global_device_ids=true | all-gather | bytes 270336 | tf_op jit(solution)/shard_map/all_gather | solution.py:75
  54.0 0.8 dynamic-update-slice
  54.8 36.8 %all-reduce = s32[512]{0:T(512)S(1)} all-reduce(s32[512]{0:T(512)S(1)} %dynamic-update-slice), channel_id=1, replica_groups=mesh['dp'=16,'grp'=2] {'dp','grp'}, use_global_device_ids=true, to_apply=%add | all-reduce | flops 512 | bytes 4096
  91.6 0.8 dynamic-update-slice.1
  92.5 41.1 %all-reduce.1 = bf16[512]{0:T(512)(128)(2,1)S(1)} all-reduce(bf16[512]{0:T(512)(128)(2,1)S(1)} %dynamic-update-slice.1), channel_id=1, replica_groups=mesh['dp'=16,'grp'=2] {'dp','grp'}, use_global_device_ids=true, to_apply=%add.1 | all-reduce | flops 512 | bytes 2048
  133.6 4.8 %multiply_convert_fusion.1 = (bf16[1024,1024]{1,0:T(8,128)(2,1)S(1)}, f32[1024,1024]{1,0:T(8,128)}) fusion(bf16[1024,512]{1,0:T(8,128)(2,1)S(1)} %copy-done, bf16[512,1024]{1,0:T(8,128)(2,1)} %param.16), kind=kOutput, calls=%fused_computation.1 | convolution fusion | flops 1078984704 | bytes 8388608 | tf_op jit(solution)/shard_map/dot_general | solution.py:16
  138.4 0.7 convolution_convert_fusion
  139.1 0.6 copy-done.7
  139.7 0.3 select_reduce_fusion
  140.0 0.8 fusion.15
  140.8 0.3 fusion.1
  141.2 0.7 multiply_convert_fusion.2
  141.8 1.2 convolution_multiply_fusion.1
  143.1 0.0 all-reduce.5.cloned.1.call-start
  143.2 0.5 fusion.2
  143.7 1.1 copy-done.8
  144.7 1.7 fusion.17
  146.5 6.1 %convolution_bitcast_fusion.1 = f32[512,1024]{0,1:T(8,128)} fusion(bf16[1024,512]{1,0:T(8,128)(2,1)S(1)} %copy-done, f32[1024,1024]{1,0:T(8,128)} %get-tuple-element.13, bf16[1024,256]{1,0:T(8,128)(2,1)S(1)} %fusion.2, bf16[1024,256]{1,0:T(8,128)(2,1)S(1)} %copy-done.6), kind=kOutput, calls=%fused_computation.13 | convolution fusion | flops 1620049920 | bytes 8388608 | tf_op jit(solution)/shard_map/dot_general | solution.py:26
  152.5 126.6 %reduce-scatter.2.cloned.1.call-done = f32[16,256]{1,0:T(8,128)} async-done(((f32[512,256]{1,0:T(8,128)}), f32[16,256]{1,0:T(8,128)}) %reduce-scatter.2.cloned.1.call-update) | async-done | bytes 16400 | tf_op jit(solution)/shard_map/reduce_scatter | solution.py:89
  279.2 2.7 convolution_bitcast_fusion
  281.9 1.3 fusion.9
  283.3 0.0 all-reduce.5.cloned.1.call-update
  283.3 0.6 convert_reduce_fusion
  283.9 38.4 %psum.36 = f32[]{:T(128)} all-reduce(f32[]{:T(128)} %convert_reduce_fusion), channel_id=1, replica_groups=mesh['dp'=16,'grp'=2] {'dp','grp'}, use_global_device_ids=true, to_apply=%region_5.6 | all-reduce | flops 1 | bytes 8 | tf_op jit(solution)/shard_map/psum | solution.py:71
  322.9 115.9 %all-reduce.5.cloned.1.call-done = (f32[512,1024]{0,1:T(8,128)}, f32[1024,256]{1,0:T(8,128)}, f32[512,1024]{0,1:T(8,128)}, f32[1024,256]{1,0:T(8,128)}) async-done(((f32[512,1024]{0,1:T(8,128)}, f32[1024,256]{1,0:T(8,128)}, f32[512,1024]{0,1:T(8,128)}, f32[1024,256]{1,0:T(8,128)}), (f32[512,1024]{0,1:T(8,128)}, f32[1024,256]{1,0:T(8,128)}, f32[512,1024]{0,1:T(8,128)}, ...) | async-done | bytes 6291472 | tf_op jit(solution)/shard_map/psum | solution.py:104
  438.8 4.0 broadcast_multiply_fusion
  442.9 2.9 copy.14
  445.8 1.8 copy.15
  447.6 3.0 broadcast_multiply_fusion.2
  (22 shorter events, 0.1 us)
Async XLA Ops:
  7.2 126.5 %copy-start = (bf16[1024,512]{1,0:T(8,128)(2,1)S(1)}, bf16[1024,512]{1,0:T(8,128)(2,1)}, u32[]{:S(2)}) copy-start(bf16[1024,512]{1,0:T(8,128)(2,1)} %param.10) | copy-start | bytes 3145732
  7.2 272.0 %reduce-scatter.2.cloned.1.call-start = ((), (), s32[]{:S(2)}) async-start(), calls=%async_computation.1 | async-start | bytes 540672 | tf_op jit(solution)/shard_map/reduce_scatter | solution.py:89
  133.6 4.8 %copy-start.6 = (bf16[1024,256]{1,0:T(8,128)(2,1)S(1)}, bf16[1024,256]{1,0:T(8,128)(2,1)}, u32[]{:S(2)}) copy-start(bf16[1024,256]{1,0:T(8,128)(2,1)} %param.17) | copy-start | bytes 1572868
  138.4 1.3 copy-start.7
  138.4 1.3 copy-start.4
  140.0 0.8 copy-start.5
  143.1 295.7 %all-reduce.5.cloned.1.call-start = ((), (), s32[]{:S(2)}) async-start(), calls=%async_computation.2 | async-start | bytes 12582912 | tf_op jit(solution)/shard_map/psum | solution.py:104
  143.2 1.6 copy-start.8
  146.5 132.7 %copy-start.1 = (bf16[1024,256]{1,0:T(8,128)(2,1)S(1)}, bf16[1024,256]{1,0:T(8,128)(2,1)}, u32[]{:S(2)}) copy-start(bf16[1024,256]{1,0:T(8,128)(2,1)} %param.19) | copy-start | bytes 1572868
  146.5 132.7 %copy-start.2 = (bf16[16,512]{1,0:T(8,128)(2,1)S(1)}, bf16[16,512]{1,0:T(8,128)(2,1)}, u32[]{:S(2)}) copy-start(bf16[16,512]{1,0:T(8,128)(2,1)} %param.13) | copy-start | bytes 49156
  279.2 2.8 copy-start.3
Sparse Core Ops, SparseCore 0:
  143.2 135.9 reduce-scatter.1
  285.8 153.0 all-reduce.4
where the time goes:
time: 458 us; the launch traced here: 457 us
  waiting for transfers between devices  243 us (53%)
  blocking collectives  160 us (35%)
  matrix products  22.6 us (5%)
  between operations  14.8 us (3%)
  other arithmetic  8.95 us (2%)
  local copies, waits for them, and re-layouts  8.09 us (2%)
    reduce_scatter x1, waiting for transfers between devices, on_device(): lax.psum_scatter(score_scale * lax.dot_general(dlogit, query_embed, (((0,...  127 us
    psum x1, waiting for transfers between devices, on_device(): lax.psum((query_in_part, query_out_part, item_in_part, item_out_part), ('...  116 us
    unnamed x2, blocking collectives  78 us
    all_gather x1, blocking collectives, on_device(): lax.all_gather(item_embed, ('dp', 'grp'), axis=0, tiled=True)  43.9 us
    psum x1, blocking collectives, on_device(): weight_total = lax.psum(weight_part, ('dp', 'grp'))  38.4 us
  transfers between devices with their start and end apart: 2, of which 2 were waited for; matrix products, arithmetic and copies ran while one was open for 2% of the time, Pallas kernels for 0%

commit v1 on v0

--- a/solution.py
+++ b/solution.py
@@ -102,7 +102,7 @@
         item_features, item_pre, item_hidden, item_w_out, item_grad
     )
     query_in_sum, query_out_sum, item_in_sum, item_out_sum = lax.psum(
-        (query_in_part, query_out_part, item_in_part, item_out_part), ("dp", "grp")
+        lax.psum((query_in_part, query_out_part, item_in_part, item_out_part), "dp"), "grp"
     )
     factor = loss_scale / weight_total
     return (

time: 458 us -> 553 us (1.21)
  waiting for transfers between devices: 243 us -> 336 us
    psum x1 -> x2, waiting for transfers between devices: 116 us -> 209 us  [the longest x1 209 us: on_device(): lax.psum((query_in_part, query_out_part, item_in_part, item_out_part), 'dp')]
  transfers between devices with their start and end apart: 2 -> 3, of which waited for: 2 -> 2; matrix products, arithmetic and copies ran while one was open for 2% -> 2% of each run, Pallas kernels for 0% -> 0%
where the time goes in v1:
time: 553 us; the launch traced here: 552 us
  waiting for transfers between devices  336 us (61%)
  blocking collectives  162 us (29%)
  matrix products  22.6 us (4%)
  between operations  14.5 us (3%)
  other arithmetic  8.96 us (2%)
  local copies, waits for them, and re-layouts  8.09 us (1%)
    psum x1, waiting for transfers between devices, on_device(): lax.psum((query_in_part, query_out_part, item_in_part, item_out_part), 'dp')  209 us
    reduce_scatter x1, waiting for transfers between devices, on_device(): lax.psum_scatter(score_scale * lax.dot_general(dlogit, query_embed, (((0,...  127 us
    unnamed x2, blocking collectives  78 us
    all_gather x1, blocking collectives, on_device(): lax.all_gather(item_embed, ('dp', 'grp'), axis=0, tiled=True)  43.9 us
    psum x1, blocking collectives, on_device(): weight_total = lax.psum(weight_part, ('dp', 'grp'))  39.6 us
  transfers between devices with their start and end apart: 3, of which 2 were waited for; matrix products, arithmetic and copies ran while one was open for 2% of the time, Pallas kernels for 0%

profile of v1, /device:TPU:0, one launch (start us, length us, event | category | flops | bytes accessed | tf_op | source)
XLA Modules:
  0.0 551.7 jit_solution(13118039173466365317)
XLA Ops:
  7.2 0.0 reduce-scatter.2.cloned.1.call-start
  7.2 1.6 fusion.16
  8.8 1.2 convolution_convert_fusion.1
  10.0 43.9 %all_gather.10 = bf16[512,256]{1,0:T(8,128)(2,1)S(1)} all-gather(bf16[16,256]{1,0:T(8,128)(2,1)S(1)} %convolution_convert_fusion.1), channel_id=1, replica_groups=mesh['dp'=16,'grp'=2] {'dp','grp'}, dimensions={0}, use_global_device_ids=true | all-gather | bytes 270336 | tf_op jit(solution)/shard_map/all_gather | solution.py:75
  54.0 0.8 dynamic-update-slice
  54.8 36.8 %all-reduce = s32[512]{0:T(512)S(1)} all-reduce(s32[512]{0:T(512)S(1)} %dynamic-update-slice), channel_id=1, replica_groups=mesh['dp'=16,'grp'=2] {'dp','grp'}, use_global_device_ids=true, to_apply=%add | all-reduce | flops 512 | bytes 4096
  91.6 0.8 dynamic-update-slice.1
  92.5 41.1 %all-reduce.1 = bf16[512]{0:T(512)(128)(2,1)S(1)} all-reduce(bf16[512]{0:T(512)(128)(2,1)S(1)} %dynamic-update-slice.1), channel_id=1, replica_groups=mesh['dp'=16,'grp'=2] {'dp','grp'}, use_global_device_ids=true, to_apply=%add.1 | all-reduce | flops 512 | bytes 2048
  133.6 4.8 multiply_convert_fusion.1
  138.4 0.7 convolution_convert_fusion
  139.1 0.6 copy-done.7
  139.7 0.3 select_reduce_fusion
  140.1 0.8 fusion.15
  140.8 0.3 fusion.1
  141.2 0.7 multiply_convert_fusion.2
  141.8 1.2 convolution_multiply_fusion.1
  143.1 0.0 all-reduce.7.cloned.1.call-start
  143.2 0.5 fusion.2
  143.7 1.1 copy-done.8
  144.7 1.7 fusion.17
  146.5 6.1 %convolution_bitcast_fusion.1 = f32[512,1024]{0,1:T(8,128)} fusion(bf16[1024,512]{1,0:T(8,128)(2,1)S(1)} %copy-done, f32[1024,1024]{1,0:T(8,128)} %get-tuple-element.17, bf16[1024,256]{1,0:T(8,128)(2,1)S(1)} %fusion.2, bf16[1024,256]{1,0:T(8,128)(2,1)S(1)} %copy-done.6), kind=kOutput, calls=%fused_computation.13 | convolution fusion | flops 1620049920 | bytes 8388608 | tf_op jit(solution)/shard_map/dot_general | solution.py:26
  152.5 126.7 %reduce-scatter.2.cloned.1.call-done = f32[16,256]{1,0:T(8,128)} async-done(((f32[512,256]{1,0:T(8,128)}), f32[16,256]{1,0:T(8,128)}) %reduce-scatter.2.cloned.1.call-update) | async-done | bytes 16400 | tf_op jit(solution)/shard_map/reduce_scatter | solution.py:89
  279.2 2.7 convolution_bitcast_fusion
  282.0 1.3 fusion.9
  283.3 0.0 all-reduce.9.cloned.1.call-start
  283.4 209.1 %all-reduce.7.cloned.1.call-done = (f32[512,1024]{0,1:T(8,128)}, f32[1024,256]{1,0:T(8,128)}, f32[512,1024]{0,1:T(8,128)}, f32[1024,256]{1,0:T(8,128)}) async-done(((f32[512,1024]{0,1:T(8,128)}, f32[1024,256]{1,0:T(8,128)}, f32[512,1024]{0,1:T(8,128)}, f32[1024,256]{1,0:T(8,128)}), (f32[512,1024]{0,1:T(8,128)}, f32[1024,256]{1,0:T(8,128)}, f32[512,1024]{0,1:T(8,128)}, ...) | async-done | bytes 6291472 | tf_op jit(solution)/shard_map/psum | solution.py:105
  492.5 0.6 convert_reduce_fusion
  493.1 39.6 %psum.65 = f32[]{:T(128)} all-reduce(f32[]{:T(128)} %convert_reduce_fusion), channel_id=1, replica_groups=mesh['dp'=16,'grp'=2] {'dp','grp'}, use_global_device_ids=true, to_apply=%region_6.7 | all-reduce | flops 1 | bytes 8 | tf_op jit(solution)/shard_map/psum | solution.py:71
  533.5 4.0 broadcast_multiply_fusion
  537.5 2.9 copy.14
  540.4 1.8 copy.15
  542.2 3.0 broadcast_multiply_fusion.2
  (25 shorter events, 0.1 us)
Async XLA Ops:
  7.2 126.5 %copy-start = (bf16[1024,512]{1,0:T(8,128)(2,1)S(1)}, bf16[1024,512]{1,0:T(8,128)(2,1)}, u32[]{:S(2)}) copy-start(bf16[1024,512]{1,0:T(8,128)(2,1)} %param.10) | copy-start | bytes 3145732
  7.2 272.0 %reduce-scatter.2.cloned.1.call-start = ((), (), s32[]{:S(2)}) async-start(), calls=%async_computation.1 | async-start | bytes 540672 | tf_op jit(solution)/shard_map/reduce_scatter | solution.py:89
  133.6 4.8 copy-start.6
  138.4 1.3 copy-start.7
  138.4 1.3 copy-start.4
  140.0 0.8 copy-start.5
  143.1 349.4 %all-reduce.7.cloned.1.call-start = ((), (), s32[]{:S(2)}) async-start(), calls=%async_computation.2 | async-start | bytes 12582912 | tf_op jit(solution)/shard_map/psum | solution.py:105
  143.2 1.6 copy-start.8
  146.5 132.8 %copy-start.1 = (bf16[1024,256]{1,0:T(8,128)(2,1)S(1)}, bf16[1024,256]{1,0:T(8,128)(2,1)}, u32[]{:S(2)}) copy-start(bf16[1024,256]{1,0:T(8,128)(2,1)} %param.19) | copy-start | bytes 1572868
  146.5 132.8 %copy-start.2 = (bf16[16,512]{1,0:T(8,128)(2,1)S(1)}, bf16[16,512]{1,0:T(8,128)(2,1)}, u32[]{:S(2)}) copy-start(bf16[16,512]{1,0:T(8,128)(2,1)} %param.13) | copy-start | bytes 49156
  279.2 2.8 copy-start.3
  283.3 250.1 %all-reduce.9.cloned.1.call-start = ((), (), s32[]{:S(2)}) async-start(), calls=%async_computation.3 | async-start | bytes 12582912 | tf_op jit(solution)/shard_map/psum | solution.py:104
Sparse Core Ops, SparseCore 0:
  143.2 135.9 reduce-scatter.1
  286.2 206.2 all-reduce.6
  495.3 31.5 all-reduce.8
